TPU v7x, 32 devices: a whole 2x2x4 slice. The times are simulated.
32 devices in a mesh: group: 4 (over y, core), dom: 8 (over z, x).
Axes of the slice: x: 2, y: 2, z: 4, core: 2. Of those that a mesh axis runs over, the one named last changes fastest.
Arguments:
- features: float32 [4096, 1024], P(('group', 'dom')), may hold values from -6 to 6
- known_mask: int32 [4096], P(('group', 'dom')), may hold values 0 or 1
- local_tile: bfloat16 [4096, 128], P(('group', 'dom')), may hold values from 0 to 1.5, as said below
- peer_tile: bfloat16 [4096, 256], P(('group', 'dom')), may hold values from 0 to 1.5, as said below
- cross_tile: bfloat16 [4096, 128], P(('group', 'dom')), may hold values from 0 to 1.5, as said below
- peer_rows: int32 [4, 8, 8, 32], P('group', 'dom'), may hold values from 0 to 127
- cross_rows: int32 [4, 8, 4, 32], P('group', 'dom'), may hold values from 0 to 127
- labels: int32 [4096], P(('group', 'dom')), may hold values from 0 to 18
- first_weight: bfloat16 [1024, 1024], replicated, may hold values from -0.1875 to 0.1875
- first_bias: float32 [1024], replicated, may hold values from -3 to 3
- second_weight: bfloat16 [1024, 19], replicated, may hold values from -60 to 60
- second_bias: float32 [19], replicated, may hold values from -3 to 3
Outputs:
- imputed: float32 [4096, 1024], P(('group', 'dom'))
- grad_first: float32 [1024, 1024], P('dom')
- grad_first_bias: float32 [1024], replicated
- grad_second: float32 [1024, 19], replicated
- grad_second_bias: float32 [19], replicated
Inputs may be any that keep to these rules, and one draw needn't show every extreme that they name: `local_tile`: each entry is 0 or lies in 0.5 to 1.5; a fraction of about 8 / 128 is nonzero. `peer_tile`: each entry is 0 or lies in 0.5 to 1.5; a fraction of about 6 / 256 is nonzero. `cross_tile`: each entry is 0 or lies in 0.5 to 1.5; a fraction of about 4 / 128 is nonzero.
All inputs are finite; a program needn't handle non-finite values. No bound on the sum of `known_mask` on one device may be relied on, other than what follows from the above.
Results may differ from a plain program's by a relative error of at most 0.0041.
Values sent between devices are 32-bit elements; how exact they have to be, the bound alone decides.
A program may use at most 64 MiB of HBM per device.

v0:
```python
import math
import jax
import jax.numpy as jnp
from jax import lax
from jax.sharding import PartitionSpec as P

SWEEPS = 3


def fetch_halos(current, peer_list, cross_list):
    width = current.shape[1]
    outgoing = current[peer_list.reshape(-1)].reshape(peer_list.shape[2], peer_list.shape[3], width)
    incoming = lax.all_to_all(outgoing, "dom", split_axis=0, concat_axis=0, tiled=True)
    leaving = current[cross_list.reshape(-1)].reshape(
        cross_list.shape[2], cross_list.shape[3], width
    )
    arriving = lax.all_to_all(leaving, "group", split_axis=0, concat_axis=0, tiled=True)
    return (incoming.reshape(-1, width), arriving.reshape(-1, width))


def local(
    features,
    known_mask,
    local_tile,
    peer_tile,
    cross_tile,
    peer_rows,
    cross_rows,
    labels,
    first_weight,
    first_bias,
    second_weight,
    second_bias,
):
    highest = lax.Precision.HIGHEST
    keep = (known_mask == 1)[:, None]
    current = jnp.where(keep, features, jnp.float32(0.0))
    local_full = local_tile.astype(jnp.float32)
    peer_full = peer_tile.astype(jnp.float32)
    cross_full = cross_tile.astype(jnp.float32)
    degree = (
        1.0 + jnp.sum(local_full, axis=1) + jnp.sum(peer_full, axis=1) + jnp.sum(cross_full, axis=1)
    )
    degree = degree[:, None]
    for sweep in range(SWEEPS):
        incoming, arriving = fetch_halos(current, peer_rows, cross_rows)
        summed = current + jnp.dot(
            local_full, current, precision=highest, preferred_element_type=jnp.float32
        )
        summed = summed + jnp.dot(
            peer_full, incoming, precision=highest, preferred_element_type=jnp.float32
        )
        summed = summed + jnp.dot(
            cross_full, arriving, precision=highest, preferred_element_type=jnp.float32
        )
        current = jnp.where(keep, features, summed / degree)
    inputs = current.astype(jnp.bfloat16)
    pre = jnp.dot(inputs, first_weight, preferred_element_type=jnp.float32) + first_bias
    sigma = jax.nn.sigmoid(pre)
    active = (pre * sigma).astype(jnp.bfloat16)
    logits = jnp.dot(active, second_weight, preferred_element_type=jnp.float32) + second_bias
    shifted = logits - jnp.max(logits, axis=1, keepdims=True)
    expo = jnp.exp(shifted)
    probs = expo / jnp.sum(expo, axis=1, keepdims=True)
    classes = second_weight.shape[1]
    onehot = (labels[:, None] == jnp.arange(classes, dtype=jnp.int32)[None, :]).astype(jnp.float32)
    total_nodes = features.shape[0] * lax.axis_size("group") * lax.axis_size("dom")
    dlogits = (probs - onehot) / jnp.float32(math.sqrt(total_nodes))
    dlogits_b = dlogits.astype(jnp.bfloat16)
    second_bias_term = jnp.sum(dlogits, axis=0)
    second_term = lax.dot_general(
        active, dlogits_b, (((0,), (0,)), ((), ())), preferred_element_type=jnp.float32
    )
    back = lax.dot_general(
        dlogits_b, second_weight, (((1,), (1,)), ((), ())), preferred_element_type=jnp.float32
    )
    dpre = (back * sigma * (1.0 + pre * (1.0 - sigma))).astype(jnp.bfloat16)
    first_bias_term = jnp.sum(dpre.astype(jnp.float32), axis=0)
    share = lax.psum_scatter(
        lax.dot_general(inputs, dpre, (((0,), (0,)), ((), ())), preferred_element_type=jnp.float32),
        "dom",
        scatter_dimension=0,
        tiled=True,
    )
    grad_first = lax.psum(share, "group")
    grad_first_bias, grad_second, grad_second_bias = lax.psum(
        (first_bias_term, second_term, second_bias_term), ("group", "dom")
    )
    return (current, grad_first, grad_first_bias, grad_second, grad_second_bias)


def solution(mesh):
    in_specs = (
        P(("group", "dom"), None),
        P(("group", "dom")),
        P(("group", "dom"), None),
        P(("group", "dom"), None),
        P(("group", "dom"), None),
        P("group", "dom", None, None),
        P("group", "dom", None, None),
        P(("group", "dom")),
        P(),
        P(),
        P(),
        P(),
    )
    out_specs = (P(("group", "dom"), None), P("dom", None), P(), P(), P())
    return jax.shard_map(local, mesh=mesh, in_specs=in_specs, out_specs=out_specs, check_vma=False)
```

profile of v0, /device:TPU:0, one launch (start us, length us, event | category | flops | bytes accessed | tf_op | source)
XLA Modules:
  0.0 363.8 jit_solution(1645723564046518858)
XLA Ops:
  13.9 4.3 %all-to-all-start.1 = ((f32[4,32,1024]{2,1,0:T(8,128)}), f32[4,32,1024]{2,1,0:T(8,128)}, u32[]{:S(2)}, u32[]{:S(2)}) async-start(f32[4,32,1024]{2,1,0:T(8,128)} %bitcast.91), calls=%async_computation.1 | async-start | bytes 1048576 | tf_op jit(solution)/shard_map/all_to_all | solution.py:17
  20.3 7.3 %all-to-all-done.1 = f32[4,32,1024]{2,1,0:T(8,128)} async-done(((f32[4,32,1024]{2,1,0:T(8,128)}), f32[4,32,1024]{2,1,0:T(8,128)}, u32[]{:S(2)}, u32[]{:S(2)}) %all-to-all-start.1) | async-done | bytes 524320 | tf_op jit(solution)/shard_map/all_to_all | solution.py:17
  27.6 6.6 %all-to-all-start = ((f32[8,32,1024]{2,1,0:T(8,128)}), f32[8,32,1024]{2,1,0:T(8,128)}, u32[]{:S(2)}, u32[]{:S(2)}) async-start(f32[8,32,1024]{2,1,0:T(8,128)} %bitcast.88), calls=%async_computation | async-start | bytes 2097152 | tf_op jit(solution)/shard_map/all_to_all | solution.py:13
  36.1 23.8 %all-to-all-done = f32[8,32,1024]{2,1,0:T(8,128)} async-done(((f32[8,32,1024]{2,1,0:T(8,128)}), f32[8,32,1024]{2,1,0:T(8,128)}, u32[]{:S(2)}, u32[]{:S(2)}) %all-to-all-start) | async-done | bytes 1048608 | tf_op jit(solution)/shard_map/all_to_all | solution.py:13
  59.9 2.2 convolution_bitcast_fusion.8
  66.1 4.1 %all-to-all-start.3 = ((f32[4,32,1024]{2,1,0:T(8,128)}), f32[4,32,1024]{2,1,0:T(8,128)}, u32[]{:S(2)}, u32[]{:S(2)}) async-start(f32[4,32,1024]{2,1,0:T(8,128)} %bitcast.93), calls=%async_computation.3 | async-start | bytes 1048576 | tf_op jit(solution)/shard_map/all_to_all | solution.py:17
  70.3 2.1 gather_fusion.2
  72.4 6.8 %all-to-all-done.3 = f32[4,32,1024]{2,1,0:T(8,128)} async-done(((f32[4,32,1024]{2,1,0:T(8,128)}), f32[4,32,1024]{2,1,0:T(8,128)}, u32[]{:S(2)}, u32[]{:S(2)}) %all-to-all-start.3) | async-done | bytes 524320 | tf_op jit(solution)/shard_map/all_to_all | solution.py:17
  79.2 4.4 %all-to-all-start.2 = ((f32[8,32,1024]{2,1,0:T(8,128)}), f32[8,32,1024]{2,1,0:T(8,128)}, u32[]{:S(2)}, u32[]{:S(2)}) async-start(f32[8,32,1024]{2,1,0:T(8,128)} %bitcast.90), calls=%async_computation.2 | async-start | bytes 2097152 | tf_op jit(solution)/shard_map/all_to_all | solution.py:13
  83.6 2.4 convolution_bitcast_fusion.2
  86.0 23.3 %all-to-all-done.2 = f32[8,32,1024]{2,1,0:T(8,128)} async-done(((f32[8,32,1024]{2,1,0:T(8,128)}), f32[8,32,1024]{2,1,0:T(8,128)}, u32[]{:S(2)}, u32[]{:S(2)}) %all-to-all-start.2) | async-done | bytes 1048608 | tf_op jit(solution)/shard_map/all_to_all | solution.py:13
  109.3 2.2 convolution_bitcast_fusion.7
  111.6 2.2 fusion.11
  116.6 4.1 %all-to-all-start.5 = ((f32[4,32,1024]{2,1,0:T(8,128)}), f32[4,32,1024]{2,1,0:T(8,128)}, u32[]{:S(2)}, u32[]{:S(2)}) async-start(f32[4,32,1024]{2,1,0:T(8,128)} %bitcast.92), calls=%async_computation.5 | async-start | bytes 1048576 | tf_op jit(solution)/shard_map/all_to_all | solution.py:17
  122.8 6.8 %all-to-all-done.5 = f32[4,32,1024]{2,1,0:T(8,128)} async-done(((f32[4,32,1024]{2,1,0:T(8,128)}), f32[4,32,1024]{2,1,0:T(8,128)}, u32[]{:S(2)}, u32[]{:S(2)}) %all-to-all-start.5) | async-done | bytes 524320 | tf_op jit(solution)/shard_map/all_to_all | solution.py:17
  129.6 4.2 %all-to-all-start.4 = ((f32[8,32,1024]{2,1,0:T(8,128)}), f32[8,32,1024]{2,1,0:T(8,128)}, u32[]{:S(2)}, u32[]{:S(2)}) async-start(f32[8,32,1024]{2,1,0:T(8,128)} %bitcast.89), calls=%async_computation.4 | async-start | bytes 2097152 | tf_op jit(solution)/shard_map/all_to_all | solution.py:13
  133.9 2.4 convolution_bitcast_fusion
  136.4 23.3 %all-to-all-done.4 = f32[8,32,1024]{2,1,0:T(8,128)} async-done(((f32[8,32,1024]{2,1,0:T(8,128)}), f32[8,32,1024]{2,1,0:T(8,128)}, u32[]{:S(2)}, u32[]{:S(2)}) %all-to-all-start.4) | async-done | bytes 1048608 | tf_op jit(solution)/shard_map/all_to_all | solution.py:13
  159.6 2.2 convolution_bitcast_fusion.6
  165.2 2.6 fusion.17
  168.8 86.5 %reduce-scatter.2.cloned.1.call-done = f32[128,1024]{1,0:T(8,128)} async-done(((f32[1024,1024]{1,0:T(8,128)}), f32[128,1024]{1,0:T(8,128)}) %reduce-scatter.2.cloned.1.call-update) | async-done | bytes 524304 | tf_op jit(solution)/shard_map/reduce_scatter | solution.py:79
  256.5 40.4 %all-reduce = (f32[1024]{0:T(1024)}, f32[19]{0:T(128)}) all-reduce(f32[1024]{0:T(1024)S(1)} %get-tuple-element.16, f32[19]{0:T(128)S(1)} %fusion.26), channel_id=1, replica_groups=mesh['group'=4,'dom'=8] {'group','dom'}, use_global_device_ids=true, to_apply=%region_8.9 | all-reduce | flops 1043 | bytes 8344 | tf_op jit(solution)/shard_map/psum | solution.py:86
  296.8 19.7 %all-reduce.6.cloned.1.call-done = f32[1024,19]{0,1:T(8,128)} async-done(((f32[1024,19]{0,1:T(8,128)}), f32[1024,19]{0,1:T(8,128)}) %all-reduce.6.cloned.1.call-update) | async-done | bytes 77840 | tf_op jit(solution)/shard_map/psum | solution.py:86
  316.6 36.4 %all-reduce.4.cloned.1.call-done = f32[128,1024]{1,0:T(8,128)} async-done(((f32[128,1024]{1,0:T(8,128)}), f32[128,1024]{1,0:T(8,128)}) %all-reduce.4.cloned.1.call-update) | async-done | bytes 524304 | tf_op jit(solution)/shard_map/psum | solution.py:85
  (60 shorter events, 27.5 us)
Async XLA Ops:
  8.0 155.8 %copy-start = (bf16[1024,1024]{1,0:T(8,128)(2,1)S(1)}, bf16[1024,1024]{1,0:T(8,128)(2,1)}, u32[]{:S(2)}) copy-start(bf16[1024,1024]{1,0:T(8,128)(2,1)} %param.20) | copy-start | bytes 6291460
  8.0 4.1 %copy-start.7 = (s32[1,1,4,32]{3,2,1,0:T(4,128)S(1)}, s32[1,1,4,32]{3,2,1,0:T(4,128)}, u32[]{:S(2)}) copy-start(s32[1,1,4,32]{3,2,1,0:T(4,128)} %param.18) | copy-start | bytes 1540
  12.3 5.9 %copy-start.5 = (s32[1,1,8,32]{3,2,1,0:T(8,128)S(1)}, s32[1,1,8,32]{3,2,1,0:T(8,128)}, u32[]{:S(2)}) copy-start(s32[1,1,8,32]{3,2,1,0:T(8,128)} %param.17) | copy-start | bytes 3076
  13.9 13.7 %all-to-all-start.1 = ((f32[4,32,1024]{2,1,0:T(8,128)}), f32[4,32,1024]{2,1,0:T(8,128)}, u32[]{:S(2)}, u32[]{:S(2)}) async-start(f32[4,32,1024]{2,1,0:T(8,128)} %bitcast.91), calls=%async_computation.1 | async-start | bytes 1048576 | tf_op jit(solution)/shard_map/all_to_all | solution.py:17
  20.3 13.9 %copy-start.2 = (bf16[128,256]{1,0:T(8,128)(2,1)S(1)}, bf16[128,256]{1,0:T(8,128)(2,1)}, u32[]{:S(2)}) copy-start(bf16[128,256]{1,0:T(8,128)(2,1)} %param.15) | copy-start | bytes 196612
  20.3 14.0 %copy-start.3 = (bf16[128,128]{1,0:T(8,128)(2,1)S(1)}, bf16[128,128]{1,0:T(8,128)(2,1)}, u32[]{:S(2)}) copy-start(bf16[128,128]{1,0:T(8,128)(2,1)} %param.16) | copy-start | bytes 98308
  20.3 14.0 %copy-start.4 = (bf16[128,128]{1,0:T(8,128)(2,1)S(1)}, bf16[128,128]{1,0:T(8,128)(2,1)}, u32[]{:S(2)}) copy-start(bf16[128,128]{1,0:T(8,128)(2,1)} %param.14) | copy-start | bytes 98308
  27.6 32.3 %all-to-all-start = ((f32[8,32,1024]{2,1,0:T(8,128)}), f32[8,32,1024]{2,1,0:T(8,128)}, u32[]{:S(2)}, u32[]{:S(2)}) async-start(f32[8,32,1024]{2,1,0:T(8,128)} %bitcast.88), calls=%async_computation | async-start | bytes 2097152 | tf_op jit(solution)/shard_map/all_to_all | solution.py:13
  66.1 13.0 %all-to-all-start.3 = ((f32[4,32,1024]{2,1,0:T(8,128)}), f32[4,32,1024]{2,1,0:T(8,128)}, u32[]{:S(2)}, u32[]{:S(2)}) async-start(f32[4,32,1024]{2,1,0:T(8,128)} %bitcast.93), calls=%async_computation.3 | async-start | bytes 1048576 | tf_op jit(solution)/shard_map/all_to_all | solution.py:17
  79.2 32.4 %copy-start.1 = (f32[128,1024]{0,1:T(8,128)S(1)}, f32[128,1024]{0,1:T(8,128)}, u32[]{:S(2)}) copy-start(f32[128,1024]{0,1:T(8,128)} %fusion.7) | copy-start | bytes 1572868
  79.2 30.1 %all-to-all-start.2 = ((f32[8,32,1024]{2,1,0:T(8,128)}), f32[8,32,1024]{2,1,0:T(8,128)}, u32[]{:S(2)}, u32[]{:S(2)}) async-start(f32[8,32,1024]{2,1,0:T(8,128)} %bitcast.90), calls=%async_computation.2 | async-start | bytes 2097152 | tf_op jit(solution)/shard_map/all_to_all | solution.py:13
  116.6 13.0 %all-to-all-start.5 = ((f32[4,32,1024]{2,1,0:T(8,128)}), f32[4,32,1024]{2,1,0:T(8,128)}, u32[]{:S(2)}, u32[]{:S(2)}) async-start(f32[4,32,1024]{2,1,0:T(8,128)} %bitcast.92), calls=%async_computation.5 | async-start | bytes 1048576 | tf_op jit(solution)/shard_map/all_to_all | solution.py:17
  129.6 30.0 %all-to-all-start.4 = ((f32[8,32,1024]{2,1,0:T(8,128)}), f32[8,32,1024]{2,1,0:T(8,128)}, u32[]{:S(2)}, u32[]{:S(2)}) async-start(f32[8,32,1024]{2,1,0:T(8,128)} %bitcast.89), calls=%async_computation.4 | async-start | bytes 2097152 | tf_op jit(solution)/shard_map/all_to_all | solution.py:13
  133.9 121.4 %reduce-scatter.2.cloned.1.call-start = ((), (), s32[]{:S(2)}) async-start(), calls=%async_computation.7 | async-start | bytes 4718592 | tf_op jit(solution)/shard_map/reduce_scatter | solution.py:79
  159.6 4.1 %copy-start.9 = (f32[1024]{0:T(1024)S(1)}, f32[1024]{0:T(1024)}, u32[]{:S(2)}) copy-start(f32[1024]{0:T(1024)} %param.21) | copy-start | bytes 12292
  163.8 0.8 copy-start.8
  163.8 0.8 copy-start.10
  163.8 1.0 copy-start.6
  167.8 148.7 %all-reduce.6.cloned.1.call-start = ((), (), s32[]{:S(2)}) async-start(), calls=%async_computation.9 | async-start | bytes 196608 | tf_op jit(solution)/shard_map/psum | solution.py:86
  168.7 184.3 %all-reduce.4.cloned.1.call-start = ((), (), s32[]{:S(2)}) async-start(), calls=%async_computation.8 | async-start | bytes 1048576 | tf_op jit(solution)/shard_map/psum | solution.py:85
Sparse Core Ops, SparseCore 0:
  168.0 87.3 reduce-scatter.1
Sparse Core Ops, SparseCore 1:
  174.5 142.0 all-reduce.5
  318.8 34.2 all-reduce.3
where the time goes:
time: 365 us; the launch traced here: 364 us
  waiting for transfers between devices  234 us (64%)
  blocking collectives  40.4 us (11%)
  starting transfers between devices  27.9 us (8%)
  matrix products  23 us (6%)
  local copies, waits for them, and re-layouts  20.8 us (6%)
  between operations  15.7 us (4%)
    reduce_scatter x1, waiting for transfers between devices, local(): lax.psum_scatter(lax.dot_general(inputs, dpre, (((0,), (0,)), ((), ())),...  86.5 us
    all_to_all x3, waiting for transfers between devices, fetch_halos(): lax.all_to_all(outgoing, 'dom', split_axis=0, concat_axis=0, tiled=True)  70.4 us
    psum x1, blocking collectives, local(): lax.psum((first_bias_term, second_term, second_bias_term), ('group', 'dom'))  40.4 us
    psum x1, waiting for transfers between devices, local(): grad_first = lax.psum(share, 'group')  36.4 us
    all_to_all x3, waiting for transfers between devices, fetch_halos(): lax.all_to_all(leaving, 'group', split_axis=0, concat_axis=0, tiled=True)  20.9 us
    psum x1, waiting for transfers between devices, local(): lax.psum((first_bias_term, second_term, second_bias_term), ('group', 'dom'))  19.7 us
    all_to_all x3, starting transfers between devices, fetch_halos(): lax.all_to_all(outgoing, 'dom', split_axis=0, concat_axis=0, tiled=True)  15.2 us
    all_to_all x3, starting transfers between devices, fetch_halos(): lax.all_to_all(leaving, 'group', split_axis=0, concat_axis=0, tiled=True)  12.6 us
  transfers between devices with their start and end apart: 9, of which 9 were waited for; matrix products, arithmetic and copies ran while one was open for 4% of the time, Pallas kernels for 0%

commit v1 on v0

--- a/solution.py
+++ b/solution.py
@@ -3,6 +3,7 @@
 import jax.numpy as jnp
 from jax import lax
 from jax.sharding import PartitionSpec as P
+from jax.lax import psum
 
 SWEEPS = 3
 
@@ -83,8 +84,8 @@
         tiled=True,
     )
     grad_first = lax.psum(share, "group")
-    grad_first_bias, grad_second, grad_second_bias = lax.psum(
-        (first_bias_term, second_term, second_bias_term), ("group", "dom")
+    grad_first_bias, grad_second, grad_second_bias = psum(
+        psum((first_bias_term, second_term, second_bias_term), axis_name="dom"), axis_name="group"
     )
     return (current, grad_first, grad_first_bias, grad_second, grad_second_bias)
 

time: 365 us -> 375 us (1.027)
  waiting for transfers between devices: 234 us -> 256 us
  blocking collectives: 40.4 us -> 26.7 us
    psum x1, waiting for transfers between devices: 19.7 us -> 65.9 us  [local(): psum((first_bias_term, second_term, second_bias_term), axis_name='dom')]
    psum x1, waiting for transfers between devices: 36.4 us -> 8.33 us  [local(): grad_first = lax.psum(share, 'group')]
    psum x1 -> x2, blocking collectives: 40.4 us -> 26.7 us  [the longest x1 20.3 us: local(): psum((first_bias_term, second_term, second_bias_term), axis_name='dom')]
    reduce_scatter x1, waiting for transfers between devices: 86.5 us -> 91 us  [local(): lax.psum_scatter(lax.dot_general(inputs, dpre, (((0,), (0,)), ((), ())),...]
  transfers between devices with their start and end apart: 9 -> 9, of which waited for: 9 -> 9; matrix products, arithmetic and copies ran while one was open for 4% -> 5% of each run, Pallas kernels for 0% -> 0%
where the time goes in v1:
time: 375 us; the launch traced here: 373 us
  waiting for transfers between devices  256 us (68%)
  starting transfers between devices  27.9 us (7%)
  matrix products  26.7 us (7%)
  blocking collectives  26.7 us (7%)
  local copies, waits for them, and re-layouts  20.6 us (5%)
  between operations  14 us (4%)
    reduce_scatter x1, waiting for transfers between devices, local(): lax.psum_scatter(lax.dot_general(inputs, dpre, (((0,), (0,)), ((), ())),...  91 us
    all_to_all x3, waiting for transfers between devices, fetch_halos(): lax.all_to_all(outgoing, 'dom', split_axis=0, concat_axis=0, tiled=True)  69.6 us
    psum x1, waiting for transfers between devices, local(): psum((first_bias_term, second_term, second_bias_term), axis_name='dom')  65.9 us
    all_to_all x3, waiting for transfers between devices, fetch_halos(): lax.all_to_all(leaving, 'group', split_axis=0, concat_axis=0, tiled=True)  20.9 us
    psum x1, blocking collectives, local(): psum((first_bias_term, second_term, second_bias_term), axis_name='dom')  20.3 us
    all_to_all x3, starting transfers between devices, fetch_halos(): lax.all_to_all(outgoing, 'dom', split_axis=0, concat_axis=0, tiled=True)  15.2 us
    all_to_all x3, starting transfers between devices, fetch_halos(): lax.all_to_all(leaving, 'group', split_axis=0, concat_axis=0, tiled=True)  12.6 us
    psum x1, waiting for transfers between devices, local(): grad_first = lax.psum(share, 'group')  8.33 us
  transfers between devices with their start and end apart: 9, of which 9 were waited for; matrix products, arithmetic and copies ran while one was open for 5% of the time, Pallas kernels for 0%

profile of v1, /device:TPU:0, one launch (start us, length us, event | category | flops | bytes accessed | tf_op | source)
XLA Modules:
  0.0 373.5 jit_solution(5187540699370002483)
XLA Ops:
  13.0 4.3 %all-to-all-start.1 = ((f32[4,32,1024]{2,1,0:T(8,128)}), f32[4,32,1024]{2,1,0:T(8,128)}, u32[]{:S(2)}, u32[]{:S(2)}) async-start(f32[4,32,1024]{2,1,0:T(8,128)} %bitcast.91), calls=%async_computation.1 | async-start | bytes 1048576 | tf_op jit(solution)/shard_map/all_to_all | solution.py:18
  19.5 7.3 %all-to-all-done.1 = f32[4,32,1024]{2,1,0:T(8,128)} async-done(((f32[4,32,1024]{2,1,0:T(8,128)}), f32[4,32,1024]{2,1,0:T(8,128)}, u32[]{:S(2)}, u32[]{:S(2)}) %all-to-all-start.1) | async-done | bytes 524320 | tf_op jit(solution)/shard_map/all_to_all | solution.py:18
  26.7 6.6 %all-to-all-start = ((f32[8,32,1024]{2,1,0:T(8,128)}), f32[8,32,1024]{2,1,0:T(8,128)}, u32[]{:S(2)}, u32[]{:S(2)}) async-start(f32[8,32,1024]{2,1,0:T(8,128)} %bitcast.88), calls=%async_computation | async-start | bytes 2097152 | tf_op jit(solution)/shard_map/all_to_all | solution.py:14
  33.6 2.4 convolution_bitcast_fusion.4
  36.0 23.0 %all-to-all-done = f32[8,32,1024]{2,1,0:T(8,128)} async-done(((f32[8,32,1024]{2,1,0:T(8,128)}), f32[8,32,1024]{2,1,0:T(8,128)}, u32[]{:S(2)}, u32[]{:S(2)}) %all-to-all-start) | async-done | bytes 1048608 | tf_op jit(solution)/shard_map/all_to_all | solution.py:14
  59.0 2.2 convolution_bitcast_fusion.8
  61.3 2.3 fusion.7
  66.4 4.1 %all-to-all-start.3 = ((f32[4,32,1024]{2,1,0:T(8,128)}), f32[4,32,1024]{2,1,0:T(8,128)}, u32[]{:S(2)}, u32[]{:S(2)}) async-start(f32[4,32,1024]{2,1,0:T(8,128)} %bitcast.93), calls=%async_computation.3 | async-start | bytes 1048576 | tf_op jit(solution)/shard_map/all_to_all | solution.py:18
  72.6 6.8 %all-to-all-done.3 = f32[4,32,1024]{2,1,0:T(8,128)} async-done(((f32[4,32,1024]{2,1,0:T(8,128)}), f32[4,32,1024]{2,1,0:T(8,128)}, u32[]{:S(2)}, u32[]{:S(2)}) %all-to-all-start.3) | async-done | bytes 524320 | tf_op jit(solution)/shard_map/all_to_all | solution.py:18
  79.4 4.4 %all-to-all-start.2 = ((f32[8,32,1024]{2,1,0:T(8,128)}), f32[8,32,1024]{2,1,0:T(8,128)}, u32[]{:S(2)}, u32[]{:S(2)}) async-start(f32[8,32,1024]{2,1,0:T(8,128)} %bitcast.90), calls=%async_computation.2 | async-start | bytes 2097152 | tf_op jit(solution)/shard_map/all_to_all | solution.py:14
  83.8 2.4 convolution_bitcast_fusion.2
  86.2 23.3 %all-to-all-done.2 = f32[8,32,1024]{2,1,0:T(8,128)} async-done(((f32[8,32,1024]{2,1,0:T(8,128)}), f32[8,32,1024]{2,1,0:T(8,128)}, u32[]{:S(2)}, u32[]{:S(2)}) %all-to-all-start.2) | async-done | bytes 1048608 | tf_op jit(solution)/shard_map/all_to_all | solution.py:14
  116.8 4.1 %all-to-all-start.5 = ((f32[4,32,1024]{2,1,0:T(8,128)}), f32[4,32,1024]{2,1,0:T(8,128)}, u32[]{:S(2)}, u32[]{:S(2)}) async-start(f32[4,32,1024]{2,1,0:T(8,128)} %bitcast.92), calls=%async_computation.5 | async-start | bytes 1048576 | tf_op jit(solution)/shard_map/all_to_all | solution.py:18
  123.0 6.8 %all-to-all-done.5 = f32[4,32,1024]{2,1,0:T(8,128)} async-done(((f32[4,32,1024]{2,1,0:T(8,128)}), f32[4,32,1024]{2,1,0:T(8,128)}, u32[]{:S(2)}, u32[]{:S(2)}) %all-to-all-start.5) | async-done | bytes 524320 | tf_op jit(solution)/shard_map/all_to_all | solution.py:18
  129.9 4.2 %all-to-all-start.4 = ((f32[8,32,1024]{2,1,0:T(8,128)}), f32[8,32,1024]{2,1,0:T(8,128)}, u32[]{:S(2)}, u32[]{:S(2)}) async-start(f32[8,32,1024]{2,1,0:T(8,128)} %bitcast.89), calls=%async_computation.4 | async-start | bytes 2097152 | tf_op jit(solution)/shard_map/all_to_all | solution.py:14
  134.2 2.4 convolution_bitcast_fusion
  136.6 23.3 %all-to-all-done.4 = f32[8,32,1024]{2,1,0:T(8,128)} async-done(((f32[8,32,1024]{2,1,0:T(8,128)}), f32[8,32,1024]{2,1,0:T(8,128)}, u32[]{:S(2)}, u32[]{:S(2)}) %all-to-all-start.4) | async-done | bytes 1048608 | tf_op jit(solution)/shard_map/all_to_all | solution.py:14
  159.9 2.2 convolution_bitcast_fusion.6
  167.8 2.6 fusion.17
  170.5 65.9 %all-reduce.6.cloned.1.call-done = f32[1024,19]{0,1:T(8,128)} async-done(((f32[1024,19]{0,1:T(8,128)}), f32[1024,19]{0,1:T(8,128)}) %all-reduce.6.cloned.1.call-update) | async-done | bytes 77840 | tf_op jit(solution)/shard_map/psum | solution.py:88
  236.4 91.0 %reduce-scatter.2.cloned.1.call-done = f32[128,1024]{1,0:T(8,128)} async-done(((f32[1024,1024]{1,0:T(8,128)}), f32[128,1024]{1,0:T(8,128)}) %reduce-scatter.2.cloned.1.call-update) | async-done | bytes 524304 | tf_op jit(solution)/shard_map/reduce_scatter | solution.py:80
  328.5 20.3 %all-reduce = (f32[1024]{0:T(1024)S(1)}, f32[19]{0:T(128)S(1)}) all-reduce(f32[1024]{0:T(1024)S(1)} %get-tuple-element.20, f32[19]{0:T(128)S(1)} %fusion.26), channel_id=1, replica_groups=mesh['group'=4,'dom'=8] {'dom'}, use_global_device_ids=true, to_apply=%region_8.9 | all-reduce | flops 1043 | bytes 8344 | tf_op jit(solution)/shard_map/psum | solution.py:88
  348.8 6.3 %all-reduce.1 = (f32[1024]{0:T(1024)}, f32[19]{0:T(128)}) all-reduce(f32[1024]{0:T(1024)S(1)} %get-tuple-element.10, f32[19]{0:T(128)S(1)} %get-tuple-element.11), channel_id=1, replica_groups=mesh['group'=4,'dom'=8] {'group'}, use_global_device_ids=true, to_apply=%region_9.10 | all-reduce | flops 1043 | bytes 8344 | tf_op jit(solution)/shard_map/psum | solution.py:87
  355.2 8.3 %all-reduce.8.cloned.1.call-done = (f32[128,1024]{1,0:T(8,128)}, f32[1024,19]{0,1:T(8,128)}) async-done(((f32[128,1024]{1,0:T(8,128)}, f32[1024,19]{0,1:T(8,128)}), (f32[128,1024]{1,0:T(8,128)}, f32[1024,19]{0,1:T(8,128)})) %all-reduce.8.cloned.1.call-update) | async-done | bytes 602128 | tf_op jit(solution)/shard_map/psum | solution.py:86
  (61 shorter events, 32.7 us)
Async XLA Ops:
  7.2 156.8 %copy-start = (bf16[1024,1024]{1,0:T(8,128)(2,1)S(1)}, bf16[1024,1024]{1,0:T(8,128)(2,1)}, u32[]{:S(2)}) copy-start(bf16[1024,1024]{1,0:T(8,128)(2,1)} %param.20) | copy-start | bytes 6291460
  7.2 4.1 %copy-start.7 = (s32[1,1,4,32]{3,2,1,0:T(4,128)S(1)}, s32[1,1,4,32]{3,2,1,0:T(4,128)}, u32[]{:S(2)}) copy-start(s32[1,1,4,32]{3,2,1,0:T(4,128)} %param.18) | copy-start | bytes 1540
  11.4 5.9 %copy-start.5 = (s32[1,1,8,32]{3,2,1,0:T(8,128)S(1)}, s32[1,1,8,32]{3,2,1,0:T(8,128)}, u32[]{:S(2)}) copy-start(s32[1,1,8,32]{3,2,1,0:T(8,128)} %param.17) | copy-start | bytes 3076
  13.0 13.7 %all-to-all-start.1 = ((f32[4,32,1024]{2,1,0:T(8,128)}), f32[4,32,1024]{2,1,0:T(8,128)}, u32[]{:S(2)}, u32[]{:S(2)}) async-start(f32[4,32,1024]{2,1,0:T(8,128)} %bitcast.91), calls=%async_computation.1 | async-start | bytes 1048576 | tf_op jit(solution)/shard_map/all_to_all | solution.py:18
  19.4 13.9 %copy-start.2 = (bf16[128,256]{1,0:T(8,128)(2,1)S(1)}, bf16[128,256]{1,0:T(8,128)(2,1)}, u32[]{:S(2)}) copy-start(bf16[128,256]{1,0:T(8,128)(2,1)} %param.15) | copy-start | bytes 196612
  19.4 14.0 %copy-start.3 = (bf16[128,128]{1,0:T(8,128)(2,1)S(1)}, bf16[128,128]{1,0:T(8,128)(2,1)}, u32[]{:S(2)}) copy-start(bf16[128,128]{1,0:T(8,128)(2,1)} %param.16) | copy-start | bytes 98308
  19.4 14.0 %copy-start.4 = (bf16[128,128]{1,0:T(8,128)(2,1)S(1)}, bf16[128,128]{1,0:T(8,128)(2,1)}, u32[]{:S(2)}) copy-start(bf16[128,128]{1,0:T(8,128)(2,1)} %param.14) | copy-start | bytes 98308
  26.7 32.3 %all-to-all-start = ((f32[8,32,1024]{2,1,0:T(8,128)}), f32[8,32,1024]{2,1,0:T(8,128)}, u32[]{:S(2)}, u32[]{:S(2)}) async-start(f32[8,32,1024]{2,1,0:T(8,128)} %bitcast.88), calls=%async_computation | async-start | bytes 2097152 | tf_op jit(solution)/shard_map/all_to_all | solution.py:14
  66.4 13.0 %all-to-all-start.3 = ((f32[4,32,1024]{2,1,0:T(8,128)}), f32[4,32,1024]{2,1,0:T(8,128)}, u32[]{:S(2)}, u32[]{:S(2)}) async-start(f32[4,32,1024]{2,1,0:T(8,128)} %bitcast.93), calls=%async_computation.3 | async-start | bytes 1048576 | tf_op jit(solution)/shard_map/all_to_all | solution.py:18
  79.4 32.4 %copy-start.1 = (f32[128,1024]{0,1:T(8,128)S(1)}, f32[128,1024]{0,1:T(8,128)}, u32[]{:S(2)}) copy-start(f32[128,1024]{0,1:T(8,128)} %fusion.7) | copy-start | bytes 1572868
  79.4 30.1 %all-to-all-start.2 = ((f32[8,32,1024]{2,1,0:T(8,128)}), f32[8,32,1024]{2,1,0:T(8,128)}, u32[]{:S(2)}, u32[]{:S(2)}) async-start(f32[8,32,1024]{2,1,0:T(8,128)} %bitcast.90), calls=%async_computation.2 | async-start | bytes 2097152 | tf_op jit(solution)/shard_map/all_to_all | solution.py:14
  116.8 13.0 %all-to-all-start.5 = ((f32[4,32,1024]{2,1,0:T(8,128)}), f32[4,32,1024]{2,1,0:T(8,128)}, u32[]{:S(2)}, u32[]{:S(2)}) async-start(f32[4,32,1024]{2,1,0:T(8,128)} %bitcast.92), calls=%async_computation.5 | async-start | bytes 1048576 | tf_op jit(solution)/shard_map/all_to_all | solution.py:18
  129.9 30.0 %all-to-all-start.4 = ((f32[8,32,1024]{2,1,0:T(8,128)}), f32[8,32,1024]{2,1,0:T(8,128)}, u32[]{:S(2)}, u32[]{:S(2)}) async-start(f32[8,32,1024]{2,1,0:T(8,128)} %bitcast.89), calls=%async_computation.4 | async-start | bytes 2097152 | tf_op jit(solution)/shard_map/all_to_all | solution.py:14
  134.1 102.3 %all-reduce.6.cloned.1.call-start = ((), (), s32[]{:S(2)}) async-start(), calls=%async_computation.8 | async-start | bytes 196608 | tf_op jit(solution)/shard_map/psum | solution.py:88
  159.8 4.1 %copy-start.9 = (f32[1024]{0:T(1024)S(1)}, f32[1024]{0:T(1024)}, u32[]{:S(2)}) copy-start(f32[1024]{0:T(1024)} %param.21) | copy-start | bytes 12292
  164.0 1.3 copy-start.8
  164.0 1.3 copy-start.10
  164.0 1.5 copy-start.6
  167.8 159.6 %reduce-scatter.2.cloned.1.call-start = ((), (), s32[]{:S(2)}) async-start(), calls=%async_computation.7 | async-start | bytes 4718592 | tf_op jit(solution)/shard_map/reduce_scatter | solution.py:80
  170.5 193.0 %all-reduce.8.cloned.1.call-start = ((), (), s32[]{:S(2)}) async-start(), calls=%async_computation.9 | async-start | bytes 1245184 | tf_op jit(solution)/shard_map/psum | solution.py:86
Sparse Core Ops, SparseCore 0:
  167.9 68.4 all-reduce.5
  240.0 87.3 reduce-scatter.1
  329.9 33.5 all-reduce.7
